TPU v7x, 32 devices: a whole 2x2x4 slice. The times are simulated.
32 devices in a mesh: seq: 16 (over z, y, core), wgt: 2 (over x).
Axes of the slice: x: 2, y: 2, z: 4, core: 2. Of those that a mesh axis runs over, the one named last changes fastest.
Arguments:
- hidden: bfloat16 [6144, 5376], P('seq', 'wgt'), may hold values from -6 to 6
- q_weight: bfloat16 [2, 5376, 2048], P(None, 'seq', 'wgt'), may hold values from -448 to 448, as said below
- k_weight: bfloat16 [2, 5376, 1024], P(None, 'seq', 'wgt'), may hold values from -448 to 448, as said below
- v_weight: bfloat16 [2, 5376, 1024], P(None, 'seq', 'wgt'), may hold values from -448 to 448, as said below
- o_weight: bfloat16 [2, 2048, 5376], P(None, 'seq', 'wgt'), may hold values from -448 to 448, as said below
- q_scale: int32 [2, 42, 16], P(None, None, 'wgt'), may hold values from 113 to 117
- k_scale: int32 [2, 42, 8], P(None, None, 'wgt'), may hold values from 113 to 117
- v_scale: int32 [2, 42, 8], P(None, None, 'wgt'), may hold values from 113 to 117
- o_scale: int32 [2, 16, 42], replicated, may hold values from 113 to 117
- in_gain: float32 [2, 5376], replicated, may hold values from 0.5 to 1.5
- post_gain: float32 [2, 5376], P(None, 'wgt'), may hold values from 0.5 to 1.5
- q_gain: float32 [2, 128], replicated, may hold values from 0.1 to 1.9
- k_gain: float32 [2, 128], replicated, may hold values from 0.1 to 1.9
- windows: int32 [2], replicated, may hold values from 512 to 1024, as said below
Outputs:
- state: bfloat16 [6144, 5376], P('seq', 'wgt')
Inputs may be any that keep to these rules, and one draw needn't show every extreme that they name: `q_weight`: every entry is a finite value of the e4m3 floating-point format: sign, 3 mantissa bits, exponents of that format. `k_weight`: every entry is a finite value of the e4m3 floating-point format. `v_weight`: every entry is a finite value of the e4m3 floating-point format. `o_weight`: every entry is a finite value of the e4m3 floating-point format. `windows`: one layer's window is exactly 1024.
All inputs are finite; a program needn't handle non-finite values.
Results may differ from a plain program's by a relative error of at most 0.0095.
Values may be sent and summed in bfloat16 or wider, within the bound.
No kernel may reach another device: no remote copies, remote signals or barrier semaphores. Data moves between devices by JAX's collectives and lax.ppermute only.
A program may use at most 192 MiB of HBM per device.

v0:
```python
import jax
import jax.numpy as jnp
from jax import lax
from jax.sharding import PartitionSpec as P

HD = 128
BLOCK = 128
WINDOW = 1024
LAYERS = 2
eps = 1e-06
query_scale = 168.0 ** (-0.5)
rope_base = 10000.0


def passed_along(array, axis, by):
    size = lax.axis_size(axis)
    pairs = [(i, i + by) for i in range(size) if 0 <= i + by < size]
    return lax.ppermute(array, axis, pairs)


def rmsnorm(values, gain):
    return values * lax.rsqrt(jnp.mean(values * values, axis=-1, keepdims=True) + eps) * gain


def rotate(values, position):
    half = values.shape[-1] // 2
    inverse = rope_base ** (-jnp.arange(half, dtype=jnp.float32) * 2.0 / values.shape[-1])
    angles = position.astype(jnp.float32)[:, None] * inverse[None, :]
    cosine = jnp.cos(angles)[:, None, :]
    sine = jnp.sin(angles)[:, None, :]
    first = values[..., :half]
    second = values[..., half:]
    return jnp.concatenate(
        [first * cosine - second * sine, second * cosine + first * sine], axis=-1
    )


def expand_scales(scale_codes):
    factor = jnp.exp2(scale_codes.astype(jnp.float32) - 127.0)
    return jnp.repeat(jnp.repeat(factor, BLOCK, axis=0), BLOCK, axis=1).astype(jnp.bfloat16)


def per_device(
    hidden,
    q_weight,
    k_weight,
    v_weight,
    o_weight,
    q_scale,
    k_scale,
    v_scale,
    o_scale,
    in_gain,
    post_gain,
    q_gain,
    k_gain,
    windows,
):
    local_rows = hidden.shape[0]
    width_share = hidden.shape[1]
    model_width = in_gain.shape[1]
    seq_index = lax.axis_index("seq")
    column_offset = lax.axis_index("wgt") * width_share
    halo_count = -(-(WINDOW - 1) // local_rows)
    position = seq_index * local_rows + jnp.arange(local_rows, dtype=jnp.int32)
    key_position = (
        seq_index * local_rows
        - halo_count * local_rows
        + jnp.arange((halo_count + 1) * local_rows, dtype=jnp.int32)
    )
    gap = position[:, None] - key_position[None, :]
    columns = column_offset + jnp.arange(width_share, dtype=jnp.int32)
    pick = (
        (columns // BLOCK)[None, :] == jnp.arange(model_width // BLOCK, dtype=jnp.int32)[:, None]
    ).astype(jnp.float32)
    gathered = (
        lax.all_gather(q_weight, "seq", axis=1, tiled=True),
        lax.all_gather(k_weight, "seq", axis=1, tiled=True),
        lax.all_gather(v_weight, "seq", axis=1, tiled=True),
        lax.all_gather(o_weight, "seq", axis=1, tiled=True),
    )
    state = hidden
    for layer_idx in range(LAYERS):
        outgoing = state
        arriving = lax.all_gather(outgoing, "wgt", axis=1, tiled=True)
        normed = rmsnorm(arriving.astype(jnp.float32), in_gain[layer_idx]).astype(jnp.bfloat16)
        tables = (
            expand_scales(q_scale[layer_idx]),
            expand_scales(k_scale[layer_idx]),
            expand_scales(v_scale[layer_idx]),
        )
        o_factor = jnp.exp2(o_scale[layer_idx].astype(jnp.float32) - 127.0)
        o_columns = jnp.dot(o_factor, pick, precision=lax.Precision.HIGHEST)
        o_table = jnp.repeat(o_columns, BLOCK, axis=0).astype(jnp.bfloat16)
        queries = jnp.dot(
            normed, gathered[0][layer_idx] * tables[0], preferred_element_type=jnp.float32
        )
        key_part = jnp.dot(
            normed, gathered[1][layer_idx] * tables[1], preferred_element_type=jnp.float32
        )
        value_part = jnp.dot(
            normed, gathered[2][layer_idx] * tables[2], preferred_element_type=jnp.float32
        )
        queries = (
            rotate(rmsnorm(queries.reshape(local_rows, -1, HD), q_gain[layer_idx]), position)
            * query_scale
        ).astype(jnp.bfloat16)
        key_heads = rotate(
            rmsnorm(key_part.reshape(local_rows, -1, HD), k_gain[layer_idx]), position
        ).astype(jnp.bfloat16)
        key_flat = key_heads.reshape(local_rows, -1)
        value_flat = value_part.astype(jnp.bfloat16)
        earlier = []
        for distance in range(1, halo_count + 1):
            earlier.insert(0, passed_along((key_flat, value_flat), "seq", distance))
        kv_local = key_flat.shape[1] // HD
        groups = queries.shape[1] // kv_local
        all_keys = jnp.concatenate([item[0] for item in earlier] + [key_flat], axis=0).reshape(
            -1, kv_local, HD
        )
        all_values = jnp.concatenate([item[1] for item in earlier] + [value_flat], axis=0).reshape(
            -1, kv_local, HD
        )
        grouped = queries.reshape(local_rows, kv_local, groups, HD)
        scores = jnp.einsum("qkgd,skd->kgqs", grouped, all_keys, preferred_element_type=jnp.float32)
        allowed = (key_position[None, :] >= 0) & (gap >= 0) & (gap < windows[layer_idx])
        scores = jnp.where(allowed, scores, -1e30)
        top = jnp.max(scores, axis=-1, keepdims=True)
        expval = jnp.exp(scores - top)
        weights = (expval / jnp.sum(expval, axis=-1, keepdims=True)).astype(jnp.bfloat16)
        mixed = jnp.einsum(
            "kgqs,skd->qkgd", weights, all_values, preferred_element_type=jnp.float32
        )
        mixed = mixed.reshape(local_rows, -1).astype(jnp.bfloat16)
        mixed_full = lax.all_gather(mixed, "wgt", axis=1, tiled=True)
        projected = jnp.dot(
            mixed_full, gathered[3][layer_idx] * o_table, preferred_element_type=jnp.float32
        )
        post_squares = lax.psum(jnp.sum(projected * projected, axis=-1), "wgt")
        post = (
            projected
            * lax.rsqrt(post_squares / model_width + eps)[:, None]
            * post_gain[layer_idx][None, :]
        )
        state = (state.astype(jnp.float32) + post).astype(jnp.bfloat16)
    return state


def solution(mesh):
    placed = (
        P("seq", "wgt"),
        P(None, "seq", "wgt"),
        P(None, "seq", "wgt"),
        P(None, "seq", "wgt"),
        P(None, "seq", "wgt"),
        P(None, None, "wgt"),
        P(None, None, "wgt"),
        P(None, None, "wgt"),
        P(),
        P(),
        P(None, "wgt"),
        P(),
        P(),
        P(),
    )
    return jax.shard_map(
        per_device, mesh=mesh, in_specs=placed, out_specs=P("seq", "wgt"), check_vma=False
    )
```

profile of v0, /device:TPU:0, one launch (start us, length us, event | category | flops | bytes accessed | tf_op | source)
XLA Modules:
  0.0 766.7 jit_solution(2744792067710179786)
XLA Ops:
  16.5 51.1 %all-gather.9.cloned.1.call-done = bf16[384,5376]{1,0:T(8,128)(2,1)} async-done(((bf16[384,2688]{1,0:T(8,128)(2,1)}), bf16[384,5376]{1,0:T(8,128)(2,1)}) %all-gather.9.cloned.1.call-update) | async-done | bytes 4128784 | tf_op jit(solution)/shard_map/all_gather | solution.py:85
  70.7 90.0 %all-gather.11.cloned.1.call-done = bf16[2,5376,512]{2,1,0:T(8,128)(2,1)} async-done(((bf16[2,336,512]{2,1,0:T(8,128)(2,1)}), bf16[2,5376,512]{2,1,0:T(8,128)(2,1)}) %all-gather.11.cloned.1.call-update) | async-done | bytes 11010064 | tf_op jit(solution)/shard_map/all_gather | solution.py:79
  161.0 6.8 broadcast_in_dim.41
  180.9 86.7 %all-gather.13.cloned.1.call-done = bf16[2,5376,512]{2,1,0:T(8,128)(2,1)} async-done(((bf16[2,336,512]{2,1,0:T(8,128)(2,1)}), bf16[2,5376,512]{2,1,0:T(8,128)(2,1)}) %all-gather.13.cloned.1.call-update) | async-done | bytes 11010064 | tf_op jit(solution)/shard_map/all_gather | solution.py:78
  267.8 6.8 broadcast_in_dim.44
  274.8 6.8 broadcast_in_dim.101
  286.4 8.2 %copy.42 = bf16[512,5376]{1,0:T(8,128)(2,1)} copy(bf16[512,5376]{0,1:T(8,128)(2,1)} %get-tuple-element.12) | data formatting | bytes 11010048 | tf_op jit(solution)/shard_map/dot_general | solution.py:98
  315.2 78.7 %all-gather.15.cloned.1.call-done = bf16[2,5376,1024]{2,1,0:T(8,128)(2,1)} async-done(((bf16[2,336,1024]{2,1,0:T(8,128)(2,1)}), bf16[2,5376,1024]{2,1,0:T(8,128)(2,1)}) %all-gather.15.cloned.1.call-update) | async-done | bytes 22020112 | tf_op jit(solution)/shard_map/all_gather | solution.py:77
  407.8 16.1 %fusion.4 = (bf16[1024,5376]{0,1:T(8,128)(2,1)}, bf16[1024,5376]{0,1:T(8,128)(2,1)}) fusion(bf16[672,8,8,128]{3,2,1,0:T(8,128)(2,1)S(1)} %bitcast.229, bf16[2,5376,1024]{2,1,0:T(8,128)(2,1)} %all-gather.15.cloned.1.call-done, bf16[672,8,8,128]{3,2,1,0:T(8,128)(2,1)S(1)} %bitcast.228), kind=kLoop, calls=%fused_computation.11 | loop fusion | flops 11010048 | bytes 66060288 | tf_op jit(solution)/shard_map/dot_general | solution.py:95
  423.9 14.4 %copy.45 = bf16[1024,5376]{1,0:T(8,128)(2,1)} copy(bf16[1024,5376]{0,1:T(8,128)(2,1)} %get-tuple-element.10) | data formatting | bytes 22020096 | tf_op jit(solution)/shard_map/dot_general | solution.py:95
  438.3 10.3 %multiply_reduce_fusion.3 = (f32[384,8]{0,1:T(8,128)S(1)}, f32[384,8,128]{0,2,1:T(8,128)S(1)}) fusion(bf16[8,128,5376]{2,1,0:T(8,128)(2,1)} %bitcast.235, f32[5376]{0:T(1024)S(1)} %get-tuple-element.6, f32[384]{0:T(512)S(1)} %add_rsqrt_fusion.7, bf16[384,5376]{1,0:T(8,128)(2,1)} %all-gather.9.cloned.1.call-done), kind=kOutput, calls=%fused_computation.85 | convolution fusion | flops 4236899328 | bytes 16747008 | tf_op jit(solution)/shard_map/dot_general | solution.py:95
  452.5 12.5 %fusion.102 = (f32[4,2,384]{2,1,0:T(2,128)S(1)}, f32[4,2,384,1536]{2,3,1,0:T(8,128)}) fusion(pred[384,1536]{0,1:T(8,128)(4,1)S(1)} %get-tuple-element.22, bf16[384,4,128]{0,2,1:T(8,128)(2,1)} %maximum_convert_fusion, bf16[384,4,128]{0,2,1:T(8,128)(2,1)} %bitcast.17, bf16[384,4,128]{0,2,1:T(8,128)(2,1)} %bitcast.16, bf16[384,4,128]{0,2,1:T(8,128)(2,1)} %bitcast.15, ...), kind=kOutput, calls=%fused_computation.180 | convolution fusion | flops 1229587968 | bytes 22622208 | tf_op jit(solution)/shard_map/sub | solution.py:129
  465.0 9.0 %fusion.48 = bf16[4,128,2,384]{3,1,2,0:T(8,128)(2,1)} fusion(bf16[1536,4,128,1]{0,2,3,1:T(8,128)(2,1)S(1)} %bitcast.252, f32[4,2,384,1536]{2,3,1,0:T(8,128)} %get-tuple-element.42, f32[4,2,384]{2,1,0:T(2,128)S(1)} %get-tuple-element.41), kind=kOutput, calls=%fused_computation.87 | convolution fusion | flops 1217789952 | bytes 21245952 | tf_op jit(solution)/shard_map/kgqs,skd->qkgd/dot_general | solution.py:131
  474.7 42.5 %all-gather.19.cloned.1.call-done = bf16[2,2048,2688]{2,1,0:T(8,128)(2,1)} async-done(((bf16[2,128,2688]{2,1,0:T(8,128)(2,1)}), bf16[2,2048,2688]{2,1,0:T(8,128)(2,1)}) %all-gather.19.cloned.1.call-update) | async-done | bytes 22020112 | tf_op jit(solution)/shard_map/all_gather | solution.py:80
  517.2 28.6 %all-gather.17.cloned.1.call-done = bf16[384,2048]{0,1:T(8,128)(2,1)} async-done(((bf16[384,1024]{0,1:T(8,128)(2,1)}), bf16[384,2048]{0,1:T(8,128)(2,1)}) %all-gather.17.cloned.1.call-update) | async-done | bytes 1572880 | tf_op jit(solution)/shard_map/all_gather | solution.py:135
  546.5 11.7 %multiply_reduce_fusion.1 = (f32[384]{0:T(512)S(1)}, f32[384,2688]{1,0:T(8,128)}) fusion(bf16[384,2048]{0,1:T(8,128)(2,1)} %all-gather.17.cloned.1.call-done, bf16[2048,2688]{1,0:T(8,128)(2,1)S(1)} %bitcast.237, bf16[2,2048,2688]{2,1,0:T(8,128)(2,1)} %all-gather.19.cloned.1.call-done), kind=kOutput, calls=%fused_computation.66 | convolution fusion | flops 4235427328 | bytes 27723264 | tf_op jit(solution)/shard_map/dot_general | solution.py:136
  568.3 8.2 %copy.47 = bf16[512,5376]{1,0:T(8,128)(2,1)} copy(bf16[512,5376]{0,1:T(8,128)(2,1)} %get-tuple-element.11) | data formatting | bytes 11010048 | tf_op jit(solution)/shard_map/dot_general | solution.py:98
  576.5 14.1 %copy.50 = bf16[1024,5376]{1,0:T(8,128)(2,1)} copy(bf16[1024,5376]{0,1:T(8,128)(2,1)} %get-tuple-element.9) | data formatting | bytes 22020096 | tf_op jit(solution)/shard_map/dot_general | solution.py:95
  590.6 33.7 %all-gather.21.cloned.1.call-done = bf16[384,5376]{1,0:T(8,128)(2,1)} async-done(((bf16[384,2688]{1,0:T(8,128)(2,1)}), bf16[384,5376]{1,0:T(8,128)(2,1)}) %all-gather.21.cloned.1.call-update) | async-done | bytes 4128784 | tf_op jit(solution)/shard_map/all_gather | solution.py:85
  642.1 6.8 broadcast_in_dim.50
  678.5 12.3 %fusion.103 = (f32[4,2,384]{2,1,0:T(2,128)S(1)}, f32[4,2,384,1536]{2,3,1,0:T(8,128)}) fusion(pred[384,1536]{0,1:T(8,128)(4,1)} %get-tuple-element.21, bf16[384,4,128]{0,2,1:T(8,128)(2,1)} %maximum_convert_fusion.1, bf16[384,4,128]{0,2,1:T(8,128)(2,1)} %bitcast.50, bf16[384,4,128]{0,2,1:T(8,128)(2,1)} %bitcast.49, bf16[384,4,128]{0,2,1:T(8,128)(2,1)} %bitcast.48, ...), kind=kOutput, calls=%fused_computation.181 | convolution fusion | flops 1229587968 | bytes 22622208 | tf_op jit(solution)/shard_map/sub | solution.py:129
  690.8 8.7 %fusion.47 = bf16[4,128,2,384]{3,1,2,0:T(8,128)(2,1)} fusion(bf16[1536,4,128,1]{0,2,3,1:T(8,128)(2,1)S(1)} %bitcast.253, f32[4,2,384,1536]{2,3,1,0:T(8,128)} %get-tuple-element.50, f32[4,2,384]{2,1,0:T(2,128)S(1)} %get-tuple-element.49), kind=kOutput, calls=%fused_computation.86 | convolution fusion | flops 1217789952 | bytes 21245952 | tf_op jit(solution)/shard_map/kgqs,skd->qkgd/dot_general | solution.py:131
  699.9 31.6 %all-gather.23.cloned.1.call-done = bf16[384,2048]{0,1:T(8,128)(2,1)} async-done(((bf16[384,1024]{0,1:T(8,128)(2,1)}), bf16[384,2048]{0,1:T(8,128)(2,1)}) %all-gather.23.cloned.1.call-update) | async-done | bytes 1572880 | tf_op jit(solution)/shard_map/all_gather | solution.py:135
  736.2 14.3 %multiply_reduce_fusion = (f32[384]{0:T(512)S(1)}, f32[384,2688]{1,0:T(8,128)}) fusion(bf16[384,2048]{0,1:T(8,128)(2,1)S(1)} %copy-done.21, bf16[2048,2688]{1,0:T(8,128)(2,1)} %bitcast.236, bf16[2,2048,2688]{2,1,0:T(8,128)(2,1)} %all-gather.19.cloned.1.call-done), kind=kOutput, calls=%fused_computation.64 | convolution fusion | flops 4235427328 | bytes 27723264 | tf_op jit(solution)/shard_map/dot_general | solution.py:136
  (166 shorter events, 142.4 us)
Async XLA Ops:
  6.6 61.1 %all-gather.9.cloned.1.call-start = ((), (), s32[]{:S(2)}) async-start(), calls=%async_computation | async-start | bytes 6193152 | tf_op jit(solution)/shard_map/all_gather | solution.py:85
  7.3 153.5 %all-gather.11.cloned.1.call-start = ((), (), s32[]{:S(2)}) async-start(), calls=%async_computation.1 | async-start | bytes 11698176 | tf_op jit(solution)/shard_map/all_gather | solution.py:79
  8.1 259.6 %all-gather.13.cloned.1.call-start = ((), (), s32[]{:S(2)}) async-start(), calls=%async_computation.2 | async-start | bytes 11698176 | tf_op jit(solution)/shard_map/all_gather | solution.py:78
  8.8 385.1 %all-gather.15.cloned.1.call-start = ((), (), s32[]{:S(2)}) async-start(), calls=%async_computation.3 | async-start | bytes 23396352 | tf_op jit(solution)/shard_map/all_gather | solution.py:77
  9.4 507.8 %all-gather.19.cloned.1.call-start = ((), (), s32[]{:S(2)}) async-start(), calls=%async_computation.5 | async-start | bytes 23396352 | tf_op jit(solution)/shard_map/all_gather | solution.py:80
  10.0 535.8 %all-gather.17.cloned.1.call-start = ((), (), s32[]{:S(2)}) async-start(), calls=%async_computation.4 | async-start | bytes 2359296 | tf_op jit(solution)/shard_map/all_gather | solution.py:135
  173.2 136.3 %collective-permute-start = (bf16[384,512]{1,0:T(8,128)(2,1)S(1)}, bf16[384,512]{1,0:T(8,128)(2,1)S(1)}, u32[]{:S(2)}, u32[]{:S(2)}) collective-permute-start(bf16[384,512]{1,0:T(8,128)(2,1)S(1)} %fusion.49), channel_id=1, source_target_pairs={{0,6},{2,8},{4,10},{6,12},{8,14},{10,16},{12,18},{14,20},{16,22},{... | collective-permute-start | bytes 1179656 | tf_op jit(solution)/shard_map/ppermute | solution.py:18
  175.4 136.3 %collective-permute-start.1 = (bf16[384,512]{1,0:T(8,128)(2,1)S(1)}, bf16[384,512]{1,0:T(8,128)(2,1)S(1)}, u32[]{:S(2)}, u32[]{:S(2)}) collective-permute-start(bf16[384,512]{1,0:T(8,128)(2,1)S(1)} %fusion.49), channel_id=1, source_target_pairs={{0,4},{2,6},{4,8},{6,10},{8,12},{10,14},{12,16},{14,18},{16,20},{1... | collective-permute-start | bytes 1179656 | tf_op jit(solution)/shard_map/ppermute | solution.py:18
  178.9 133.5 %collective-permute-start.2 = (bf16[384,512]{1,0:T(8,128)(2,1)S(1)}, bf16[384,512]{1,0:T(8,128)(2,1)}, u32[]{:S(2)}, u32[]{:S(2)}) collective-permute-start(bf16[384,512]{1,0:T(8,128)(2,1)S(1)} %fusion.49), channel_id=1, source_target_pairs={{0,2},{2,4},{4,6},{6,8},{8,10},{10,12},{12,14},{14,16},{16,18},{18... | collective-permute-start | bytes 1179656 | tf_op jit(solution)/shard_map/ppermute | solution.py:18
  302.3 150.1 %collective-permute-start.3 = (bf16[384,512]{0,1:T(8,128)(2,1)}, bf16[384,512]{0,1:T(8,128)(2,1)}, u32[]{:S(2)}, u32[]{:S(2)}) collective-permute-start(bf16[384,512]{0,1:T(8,128)(2,1)} %bitcast.14), channel_id=1, source_target_pairs={{0,6},{2,8},{4,10},{6,12},{8,14},{10,16},{12,18},{14,20},{16,22},{... | collective-permute-start | bytes 1179656 | tf_op jit(solution)/shard_map/ppermute | solution.py:18
  305.3 147.1 %collective-permute-start.4 = (bf16[384,512]{0,1:T(8,128)(2,1)}, bf16[384,512]{0,1:T(8,128)(2,1)}, u32[]{:S(2)}, u32[]{:S(2)}) collective-permute-start(bf16[384,512]{0,1:T(8,128)(2,1)} %bitcast.14), channel_id=1, source_target_pairs={{0,4},{2,6},{4,8},{6,10},{8,12},{10,14},{12,16},{14,18},{16,20},{1... | collective-permute-start | bytes 1179656 | tf_op jit(solution)/shard_map/ppermute | solution.py:18
  309.5 143.0 %collective-permute-start.5 = (bf16[384,512]{0,1:T(8,128)(2,1)}, bf16[384,512]{0,1:T(8,128)(2,1)}, u32[]{:S(2)}, u32[]{:S(2)}) collective-permute-start(bf16[384,512]{0,1:T(8,128)(2,1)} %bitcast.14), channel_id=1, source_target_pairs={{0,2},{2,4},{4,6},{6,8},{8,10},{10,12},{12,14},{14,16},{16,18},{18... | collective-permute-start | bytes 1179656 | tf_op jit(solution)/shard_map/ppermute | solution.py:18
  474.0 150.3 %all-gather.21.cloned.1.call-start = ((), (), s32[]{:S(2)}) async-start(), calls=%async_computation.6 | async-start | bytes 6193152 | tf_op jit(solution)/shard_map/all_gather | solution.py:85
  474.3 72.2 %copy-start.11 = (s32[2688]{0:T(1024)}, s32[2688]{0:T(1024)S(1)}, u32[]{:S(2)}) copy-start(s32[2688]{0:T(1024)S(1)} %add_select_fusion) | copy-start | bytes 32260
  568.1 163.4 %all-gather.23.cloned.1.call-start = ((), (), s32[]{:S(2)}) async-start(), calls=%async_computation.7 | async-start | bytes 2359296 | tf_op jit(solution)/shard_map/all_gather | solution.py:135
  634.0 44.4 %collective-permute-start.9 = (bf16[384,512]{0,1:T(8,128)(2,1)}, bf16[384,512]{0,1:T(8,128)(2,1)}, u32[]{:S(2)}, u32[]{:S(2)}) collective-permute-start(bf16[384,512]{0,1:T(8,128)(2,1)} %bitcast.47), channel_id=1, source_target_pairs={{0,6},{2,8},{4,10},{6,12},{8,14},{10,16},{12,18},{14,20},{16,22},{... | collective-permute-start | bytes 1179656 | tf_op jit(solution)/shard_map/ppermute | solution.py:18
  637.4 41.0 %collective-permute-start.10 = (bf16[384,512]{0,1:T(8,128)(2,1)}, bf16[384,512]{0,1:T(8,128)(2,1)}, u32[]{:S(2)}, u32[]{:S(2)}) collective-permute-start(bf16[384,512]{0,1:T(8,128)(2,1)} %bitcast.47), channel_id=1, source_target_pairs={{0,4},{2,6},{4,8},{6,10},{8,12},{10,14},{12,16},{14,18},{16,20},{1... | collective-permute-start | bytes 1179656 | tf_op jit(solution)/shard_map/ppermute | solution.py:18
  642.1 21.4 %slice-start = ((s8[11010048]{0:T(1024)(128)(4,1)}), s8[4194304]{0:T(1024)(128)(4,1)S(1)}, s32[]{:S(2)}) async-start(s8[11010048]{0:T(1024)(128)(4,1)} %bitcast.232), calls=%async_computation.8 | async-start | bytes 8388608
  648.9 14.6 %slice-start.1 = ((s8[11010048]{0:T(1024)(128)(4,1)}), s8[4194304]{0:T(1024)(128)(4,1)S(1)}, s32[]{:S(2)}) async-start(s8[11010048]{0:T(1024)(128)(4,1)} %bitcast.232), calls=%async_computation.9 | async-start | bytes 8388608
  654.9 14.9 %collective-permute-start.6 = (bf16[384,512]{1,0:T(8,128)(2,1)}, bf16[384,512]{1,0:T(8,128)(2,1)S(1)}, u32[]{:S(2)}, u32[]{:S(2)}) collective-permute-start(bf16[384,512]{1,0:T(8,128)(2,1)} %fusion.50), channel_id=1, source_target_pairs={{0,6},{2,8},{4,10},{6,12},{8,14},{10,16},{12,18},{14,20},{16,22},{... | collective-permute-start | bytes 1179656 | tf_op jit(solution)/shard_map/ppermute | solution.py:18
  657.1 18.2 %collective-permute-start.7 = (bf16[384,512]{1,0:T(8,128)(2,1)}, bf16[384,512]{1,0:T(8,128)(2,1)}, u32[]{:S(2)}, u32[]{:S(2)}) collective-permute-start(bf16[384,512]{1,0:T(8,128)(2,1)} %fusion.50), channel_id=1, source_target_pairs={{0,4},{2,6},{4,8},{6,10},{8,12},{10,14},{12,16},{14,18},{16,20},{1... | collective-permute-start | bytes 1179656 | tf_op jit(solution)/shard_map/ppermute | solution.py:18
  661.2 14.1 %collective-permute-start.8 = (bf16[384,512]{1,0:T(8,128)(2,1)}, bf16[384,512]{1,0:T(8,128)(2,1)}, u32[]{:S(2)}, u32[]{:S(2)}) collective-permute-start(bf16[384,512]{1,0:T(8,128)(2,1)} %fusion.50), channel_id=1, source_target_pairs={{0,2},{2,4},{4,6},{6,8},{8,10},{10,12},{12,14},{14,16},{16,18},{18... | collective-permute-start | bytes 1179656 | tf_op jit(solution)/shard_map/ppermute | solution.py:18
  669.8 8.6 %collective-permute-start.11 = (bf16[384,512]{0,1:T(8,128)(2,1)}, bf16[384,512]{0,1:T(8,128)(2,1)}, u32[]{:S(2)}, u32[]{:S(2)}) collective-permute-start(bf16[384,512]{0,1:T(8,128)(2,1)} %bitcast.47), channel_id=1, source_target_pairs={{0,2},{2,4},{4,6},{6,8},{8,10},{10,12},{12,14},{14,16},{16,18},{18... | collective-permute-start | bytes 1179656 | tf_op jit(solution)/shard_map/ppermute | solution.py:18
  736.2 19.2 %copy-start = (bf16[384,2688]{1,0:T(8,128)(2,1)S(1)}, bf16[384,2688]{1,0:T(8,128)(2,1)}, u32[]{:S(2)}) copy-start(bf16[384,2688]{1,0:T(8,128)(2,1)} %add_convert_fusion.1) | copy-start | bytes 6193156
  (23 other events, 152.4 us)
Sparse Core Ops, SparseCore 0:
  8.9 58.6 all-gather.8
  69.9 90.7 all-gather.10
  163.1 104.5 all-gather.12
  269.0 124.8 all-gather.14
  395.3 121.8 all-gather.18
  518.6 27.1 all-gather.16
  568.2 55.9 all-gather.20
  699.7 31.7 all-gather.22
where the time goes:
time: 775 us; the launch traced here: 767 us
  waiting for transfers between devices  446 us (58%)
  matrix products  109 us (14%)
  local copies, waits for them, and re-layouts  105 us (14%)
  other arithmetic  46 us (6%)
  starting transfers between devices  37.1 us (5%)
  between operations  14.4 us (2%)
  blocking collectives  9.82 us (1%)
    all_gather x1, waiting for transfers between devices, per_device(): lax.all_gather(v_weight, 'seq', axis=1, tiled=True)  90 us
    all_gather x1, waiting for transfers between devices, per_device(): lax.all_gather(k_weight, 'seq', axis=1, tiled=True)  86.7 us
    all_gather x2, waiting for transfers between devices, per_device(): arriving = lax.all_gather(outgoing, 'wgt', axis=1, tiled=True)  84.8 us
    all_gather x1, waiting for transfers between devices, per_device(): lax.all_gather(q_weight, 'seq', axis=1, tiled=True)  78.7 us
    all_gather x2, waiting for transfers between devices, per_device(): mixed_full = lax.all_gather(mixed, 'wgt', axis=1, tiled=True)  60.2 us
    all_gather x1, waiting for transfers between devices, per_device(): lax.all_gather(o_weight, 'seq', axis=1, tiled=True)  42.5 us
    broadcast_in_dim x6, local copies, waits for them, and re-layouts, expand_scales(): jnp.repeat(jnp.repeat(factor, BLOCK, axis=0), BLOCK, axis=1)  40.7 us
    ppermute x12, starting transfers between devices, passed_along(): return lax.ppermute(array, axis, pairs)  36.6 us
  transfers between devices with their start and end apart: 20, of which 8 were waited for; matrix products, arithmetic and copies ran while one was open for 24% of the time, Pallas kernels for 0%

commit v1 on v0

--- a/solution.py
+++ b/solution.py
@@ -82,7 +82,7 @@
     state = hidden
     for layer_idx in range(LAYERS):
         outgoing = state
-        arriving = lax.all_gather(outgoing, "wgt", axis=1, tiled=True)
+        arriving = jnp.concatenate(lax.all_gather(outgoing, axis_name="wgt"), axis=1)
         normed = rmsnorm(arriving.astype(jnp.float32), in_gain[layer_idx]).astype(jnp.bfloat16)
         tables = (
             expand_scales(q_scale[layer_idx]),

time: 775 us -> 799 us (1.031)
  local copies, waits for them, and re-layouts: 105 us -> 182 us
  waiting for transfers between devices: 446 us -> 380 us
    convert_element_type x0 -> x8, local copies, waits for them, and re-layouts: none -> 57.5 us  [the longest x6 37.2 us: per_device(): rmsnorm(arriving.astype(jnp.float32), in_gain[layer_idx])]
    all_gather x2, waiting for transfers between devices: 84.8 us -> 31.4 us  [per_device(): lax.all_gather(outgoing, axis_name='wgt')]
    all_gather x1, waiting for transfers between devices: 90 us -> 65.6 us  [per_device(): lax.all_gather(v_weight, 'seq', axis=1, tiled=True)]
    broadcast_in_dim x6, local copies, waits for them, and re-layouts: 40.7 us -> 59.3 us  [expand_scales(): jnp.repeat(jnp.repeat(factor, BLOCK, axis=0), BLOCK, axis=1)]
  transfers between devices with their start and end apart: 20 -> 20, of which waited for: 8 -> 8; matrix products, arithmetic and copies ran while one was open for 24% -> 32% of each run, Pallas kernels for 0% -> 0%
where the time goes in v1:
time: 799 us; the launch traced here: 788 us
  waiting for transfers between devices  380 us (48%)
  local copies, waits for them, and re-layouts  182 us (23%)
  matrix products  112 us (14%)
  other arithmetic  52.7 us (7%)
  starting transfers between devices  37.3 us (5%)
  between operations  14.6 us (2%)
  blocking collectives  9.82 us (1%)
    all_gather x1, waiting for transfers between devices, per_device(): lax.all_gather(k_weight, 'seq', axis=1, tiled=True)  93.5 us
    all_gather x1, waiting for transfers between devices, per_device(): lax.all_gather(q_weight, 'seq', axis=1, tiled=True)  78.8 us
    all_gather x1, waiting for transfers between devices, per_device(): lax.all_gather(v_weight, 'seq', axis=1, tiled=True)  65.6 us
    all_gather x2, waiting for transfers between devices, per_device(): mixed_full = lax.all_gather(mixed, 'wgt', axis=1, tiled=True)  65.4 us
    broadcast_in_dim x6, local copies, waits for them, and re-layouts, expand_scales(): jnp.repeat(jnp.repeat(factor, BLOCK, axis=0), BLOCK, axis=1)  59.3 us
    all_gather x1, waiting for transfers between devices, per_device(): lax.all_gather(o_weight, 'seq', axis=1, tiled=True)  42.2 us
    convert_element_type x6, local copies, waits for them, and re-layouts, per_device(): rmsnorm(arriving.astype(jnp.float32), in_gain[layer_idx])  37.2 us
    ppermute x12, starting transfers between devices, passed_along(): return lax.ppermute(array, axis, pairs)  36.4 us
  transfers between devices with their start and end apart: 20, of which 8 were waited for; matrix products, arithmetic and copies ran while one was open for 32% of the time, Pallas kernels for 0%

profile of v1, /device:TPU:0, one launch (start us, length us, event | category | flops | bytes accessed | tf_op | source)
XLA Modules:
  0.0 788.0 jit_solution(11724956123383834794)
XLA Ops:
  10.9 16.1 %broadcast_in_dim.41 = bf16[5376,4,128]{2,1,0:T(4,128)(2,1)} broadcast(bf16[5376,4]{1,0:T(8,128)(2,1)S(1)} %bitcast.234), dimensions={0,1} | broadcast | bytes 5548032 | tf_op jit(solution)/shard_map/broadcast_in_dim | solution.py:40
  27.0 10.2 %convert_element_type.236 = bf16[1,5376,512]{2,1,0:T(8,128)(2,1)} reshape(bf16[5376,4,128]{2,1,0:T(4,128)(2,1)} %broadcast_in_dim.41) | data formatting | bytes 11010048 | tf_op jit(solution)/shard_map/convert_element_type | solution.py:40
  42.9 24.8 %all-gather.23.cloned.1.call-done = bf16[768,2688]{1,0:T(8,128)(2,1)} async-done(((bf16[384,2688]{1,0:T(8,128)(2,1)}), bf16[768,2688]{1,0:T(8,128)(2,1)}) %all-gather.23.cloned.1.call-update) | async-done | bytes 4128784 | tf_op jit(solution)/shard_map/all_gather | solution.py:85
  80.6 10.0 %reshape.365 = bf16[384,5376,1]{1,0,2:T(8,128)(2,1)} reshape(bf16[384,2,2688]{2,1,0:T(2,128)(2,1)} %copy.15) | data formatting | bytes 8257536 | tf_op jit(solution)/shard_map/convert_element_type | solution.py:86
  95.1 65.6 %all-gather.11.cloned.1.call-done = bf16[2,5376,512]{2,1,0:T(8,128)(2,1)} async-done(((bf16[2,336,512]{2,1,0:T(8,128)(2,1)}), bf16[2,5376,512]{2,1,0:T(8,128)(2,1)}) %all-gather.11.cloned.1.call-update) | async-done | bytes 11010064 | tf_op jit(solution)/shard_map/all_gather | solution.py:79
  176.3 93.5 %all-gather.13.cloned.1.call-done = bf16[2,5376,512]{2,1,0:T(8,128)(2,1)} async-done(((bf16[2,336,512]{2,1,0:T(8,128)(2,1)}), bf16[2,5376,512]{2,1,0:T(8,128)(2,1)}) %all-gather.13.cloned.1.call-update) | async-done | bytes 11010064 | tf_op jit(solution)/shard_map/all_gather | solution.py:78
  288.5 8.4 %copy.44 = bf16[512,5376]{1,0:T(8,128)(2,1)} copy(bf16[512,5376]{0,1:T(8,128)(2,1)} %get-tuple-element.12) | data formatting | bytes 11010048 | tf_op jit(solution)/shard_map/dot_general | solution.py:98
  317.3 78.8 %all-gather.15.cloned.1.call-done = bf16[2,5376,1024]{2,1,0:T(8,128)(2,1)} async-done(((bf16[2,336,1024]{2,1,0:T(8,128)(2,1)}), bf16[2,5376,1024]{2,1,0:T(8,128)(2,1)}) %all-gather.15.cloned.1.call-update) | async-done | bytes 22020112 | tf_op jit(solution)/shard_map/all_gather | solution.py:77
  410.0 16.1 %fusion.4 = (bf16[1024,5376]{0,1:T(8,128)(2,1)}, bf16[1024,5376]{0,1:T(8,128)(2,1)}) fusion(bf16[672,8,8,128]{3,2,1,0:T(8,128)(2,1)S(1)} %bitcast.215, bf16[2,5376,1024]{2,1,0:T(8,128)(2,1)} %all-gather.15.cloned.1.call-done, bf16[672,8,8,128]{3,2,1,0:T(8,128)(2,1)S(1)} %bitcast.214), kind=kLoop, calls=%fused_computation.11 | loop fusion | flops 11010048 | bytes 66060288 | tf_op jit(solution)/shard_map/dot_general | solution.py:95
  426.1 14.8 %copy.47 = bf16[1024,5376]{1,0:T(8,128)(2,1)} copy(bf16[1024,5376]{0,1:T(8,128)(2,1)} %get-tuple-element.10) | data formatting | bytes 22020096 | tf_op jit(solution)/shard_map/dot_general | solution.py:95
  441.0 10.0 %multiply_reduce_fusion.3 = (f32[384,8]{0,1:T(8,128)S(1)}, f32[384,8,128]{0,2,1:T(8,128)S(1)}) fusion(bf16[384,5376,1]{1,0,2:T(8,128)(2,1)} %reshape.365, bf16[8,128,5376]{2,1,0:T(8,128)(2,1)} %bitcast.226), kind=kOutput, calls=%fused_computation.75 | convolution fusion | flops 4228641792 | bytes 16723968 | tf_op jit(solution)/shard_map/dot_general | solution.py:95
  454.8 12.5 %fusion.98 = (f32[4,2,384]{2,1,0:T(2,128)S(1)}, f32[4,2,384,1536]{2,3,1,0:T(8,128)}) fusion(pred[384,1536]{0,1:T(8,128)(4,1)S(1)} %get-tuple-element.26, bf16[384,4,128]{0,2,1:T(8,128)(2,1)} %maximum_convert_fusion, bf16[384,4,128]{0,2,1:T(8,128)(2,1)} %bitcast.19, bf16[384,4,128]{0,2,1:T(8,128)(2,1)} %bitcast.18, bf16[384,4,128]{0,2,1:T(8,128)(2,1)} %bitcast.17, ...), kind=kOutput, calls=%fused_computation.174 | convolution fusion | flops 1229587968 | bytes 22622208 | tf_op jit(solution)/shard_map/sub | solution.py:129
  467.3 9.0 %fusion.42 = bf16[4,128,2,384]{3,1,2,0:T(8,128)(2,1)} fusion(bf16[1536,4,128,1]{0,2,3,1:T(8,128)(2,1)S(1)} %bitcast.244, f32[4,2,384,1536]{2,3,1,0:T(8,128)} %get-tuple-element.46, f32[4,2,384]{2,1,0:T(2,128)S(1)} %get-tuple-element.45), kind=kOutput, calls=%fused_computation.77 | convolution fusion | flops 1217789952 | bytes 21245952 | tf_op jit(solution)/shard_map/kgqs,skd->qkgd/dot_general | solution.py:131
  477.2 42.2 %all-gather.19.cloned.1.call-done = bf16[2,2048,2688]{2,1,0:T(8,128)(2,1)} async-done(((bf16[2,128,2688]{2,1,0:T(8,128)(2,1)}), bf16[2,2048,2688]{2,1,0:T(8,128)(2,1)}) %all-gather.19.cloned.1.call-update) | async-done | bytes 22020112 | tf_op jit(solution)/shard_map/all_gather | solution.py:80
  519.4 28.6 %all-gather.17.cloned.1.call-done = bf16[384,2048]{0,1:T(8,128)(2,1)} async-done(((bf16[384,1024]{0,1:T(8,128)(2,1)}), bf16[384,2048]{0,1:T(8,128)(2,1)}) %all-gather.17.cloned.1.call-update) | async-done | bytes 1572880 | tf_op jit(solution)/shard_map/all_gather | solution.py:135
  548.7 11.7 %multiply_reduce_fusion.1 = (f32[384]{0:T(512)S(1)}, f32[384,2688]{1,0:T(8,128)}) fusion(bf16[384,2048]{0,1:T(8,128)(2,1)} %all-gather.17.cloned.1.call-done, bf16[2048,2688]{1,0:T(8,128)(2,1)S(1)} %bitcast.227, bf16[2,2048,2688]{2,1,0:T(8,128)(2,1)} %all-gather.19.cloned.1.call-done), kind=kOutput, calls=%fused_computation.56 | convolution fusion | flops 4235427328 | bytes 27723264 | tf_op jit(solution)/shard_map/dot_general | solution.py:136
  570.8 16.1 %broadcast_in_dim.50 = bf16[5376,4,128]{2,1,0:T(4,128)(2,1)} broadcast(bf16[5376,4]{1,0:T(8,128)(2,1)S(1)} %bitcast.237), dimensions={0,1} | broadcast | bytes 5548032 | tf_op jit(solution)/shard_map/broadcast_in_dim | solution.py:40
  586.9 10.1 %convert_element_type.263 = bf16[1,5376,512]{2,1,0:T(8,128)(2,1)} reshape(bf16[5376,4,128]{2,1,0:T(4,128)(2,1)} %broadcast_in_dim.50) | data formatting | bytes 11010048 | tf_op jit(solution)/shard_map/convert_element_type | solution.py:40
  605.0 14.7 %copy.52 = bf16[1024,5376]{1,0:T(8,128)(2,1)} copy(bf16[1024,5376]{0,1:T(8,128)(2,1)} %get-tuple-element.9) | data formatting | bytes 22020096 | tf_op jit(solution)/shard_map/dot_general | solution.py:95
  639.3 9.9 %reshape.368 = bf16[384,5376,1]{1,0,2:T(8,128)(2,1)} reshape(bf16[384,2,2688]{2,1,0:T(2,128)(2,1)} %copy.26) | data formatting | bytes 8257536 | tf_op jit(solution)/shard_map/convert_element_type | solution.py:86
  694.3 12.3 %fusion.99 = (f32[4,2,384]{2,1,0:T(2,128)S(1)}, f32[4,2,384,1536]{2,3,1,0:T(8,128)}) fusion(pred[384,1536]{0,1:T(8,128)(4,1)} %get-tuple-element.25, bf16[384,4,128]{0,2,1:T(8,128)(2,1)} %maximum_convert_fusion.1, bf16[384,4,128]{0,2,1:T(8,128)(2,1)} %bitcast.54, bf16[384,4,128]{0,2,1:T(8,128)(2,1)} %bitcast.53, bf16[384,4,128]{0,2,1:T(8,128)(2,1)} %bitcast.52, ...), kind=kOutput, calls=%fused_computation.175 | convolution fusion | flops 1229587968 | bytes 22622208 | tf_op jit(solution)/shard_map/sub | solution.py:129
  706.6 8.7 %fusion.41 = bf16[4,128,2,384]{3,1,2,0:T(8,128)(2,1)} fusion(bf16[1536,4,128,1]{0,2,3,1:T(8,128)(2,1)S(1)} %bitcast.245, f32[4,2,384,1536]{2,3,1,0:T(8,128)} %get-tuple-element.54, f32[4,2,384]{2,1,0:T(2,128)S(1)} %get-tuple-element.53), kind=kOutput, calls=%fused_computation.76 | convolution fusion | flops 1217789952 | bytes 21245952 | tf_op jit(solution)/shard_map/kgqs,skd->qkgd/dot_general | solution.py:131
  715.6 36.8 %all-gather.21.cloned.1.call-done = bf16[384,2048]{0,1:T(8,128)(2,1)} async-done(((bf16[384,1024]{0,1:T(8,128)(2,1)}), bf16[384,2048]{0,1:T(8,128)(2,1)}) %all-gather.21.cloned.1.call-update) | async-done | bytes 1572880 | tf_op jit(solution)/shard_map/all_gather | solution.py:135
  757.2 14.3 %multiply_reduce_fusion = (f32[384]{0:T(512)S(1)}, f32[384,2688]{1,0:T(8,128)}) fusion(bf16[384,2048]{0,1:T(8,128)(2,1)S(1)} %copy-done.23, bf16[2048,2688]{1,0:T(8,128)(2,1)} %bitcast.225, bf16[2,2048,2688]{2,1,0:T(8,128)(2,1)} %all-gather.19.cloned.1.call-done), kind=kOutput, calls=%fused_computation.54 | convolution fusion | flops 4235427328 | bytes 27723264 | tf_op jit(solution)/shard_map/dot_general | solution.py:136
  (187 shorter events, 198.3 us)
Async XLA Ops:
  6.5 61.1 %all-gather.23.cloned.1.call-start = ((), (), s32[]{:S(2)}) async-start(), calls=%async_computation.6 | async-start | bytes 6193152 | tf_op jit(solution)/shard_map/all_gather | solution.py:85
  7.3 153.5 %all-gather.11.cloned.1.call-start = ((), (), s32[]{:S(2)}) async-start(), calls=%async_computation | async-start | bytes 11698176 | tf_op jit(solution)/shard_map/all_gather | solution.py:79
  8.0 261.8 %all-gather.13.cloned.1.call-start = ((), (), s32[]{:S(2)}) async-start(), calls=%async_computation.1 | async-start | bytes 11698176 | tf_op jit(solution)/shard_map/all_gather | solution.py:78
  8.8 387.3 %all-gather.15.cloned.1.call-start = ((), (), s32[]{:S(2)}) async-start(), calls=%async_computation.2 | async-start | bytes 23396352 | tf_op jit(solution)/shard_map/all_gather | solution.py:77
  9.3 510.0 %all-gather.19.cloned.1.call-start = ((), (), s32[]{:S(2)}) async-start(), calls=%async_computation.4 | async-start | bytes 23396352 | tf_op jit(solution)/shard_map/all_gather | solution.py:80
  9.9 538.0 %all-gather.17.cloned.1.call-start = ((), (), s32[]{:S(2)}) async-start(), calls=%async_computation.3 | async-start | bytes 2359296 | tf_op jit(solution)/shard_map/all_gather | solution.py:135
  168.4 143.3 %collective-permute-start = (bf16[384,512]{1,0:T(8,128)(2,1)S(1)}, bf16[384,512]{1,0:T(8,128)(2,1)S(1)}, u32[]{:S(2)}, u32[]{:S(2)}) collective-permute-start(bf16[384,512]{1,0:T(8,128)(2,1)S(1)} %fusion.43), channel_id=1, source_target_pairs={{0,6},{2,8},{4,10},{6,12},{8,14},{10,16},{12,18},{14,20},{16,22},{... | collective-permute-start | bytes 1179656 | tf_op jit(solution)/shard_map/ppermute | solution.py:18
  170.8 143.0 %collective-permute-start.1 = (bf16[384,512]{1,0:T(8,128)(2,1)S(1)}, bf16[384,512]{1,0:T(8,128)(2,1)S(1)}, u32[]{:S(2)}, u32[]{:S(2)}) collective-permute-start(bf16[384,512]{1,0:T(8,128)(2,1)S(1)} %fusion.43), channel_id=1, source_target_pairs={{0,4},{2,6},{4,8},{6,10},{8,12},{10,14},{12,16},{14,18},{16,20},{1... | collective-permute-start | bytes 1179656 | tf_op jit(solution)/shard_map/ppermute | solution.py:18
  174.2 140.3 %collective-permute-start.2 = (bf16[384,512]{1,0:T(8,128)(2,1)S(1)}, bf16[384,512]{1,0:T(8,128)(2,1)}, u32[]{:S(2)}, u32[]{:S(2)}) collective-permute-start(bf16[384,512]{1,0:T(8,128)(2,1)S(1)} %fusion.43), channel_id=1, source_target_pairs={{0,2},{2,4},{4,6},{6,8},{8,10},{10,12},{12,14},{14,16},{16,18},{18... | collective-permute-start | bytes 1179656 | tf_op jit(solution)/shard_map/ppermute | solution.py:18
  304.4 150.4 %collective-permute-start.3 = (bf16[384,512]{0,1:T(8,128)(2,1)}, bf16[384,512]{0,1:T(8,128)(2,1)}, u32[]{:S(2)}, u32[]{:S(2)}) collective-permute-start(bf16[384,512]{0,1:T(8,128)(2,1)} %bitcast.16), channel_id=1, source_target_pairs={{0,6},{2,8},{4,10},{6,12},{8,14},{10,16},{12,18},{14,20},{16,22},{... | collective-permute-start | bytes 1179656 | tf_op jit(solution)/shard_map/ppermute | solution.py:18
  307.4 147.4 %collective-permute-start.4 = (bf16[384,512]{0,1:T(8,128)(2,1)}, bf16[384,512]{0,1:T(8,128)(2,1)}, u32[]{:S(2)}, u32[]{:S(2)}) collective-permute-start(bf16[384,512]{0,1:T(8,128)(2,1)} %bitcast.16), channel_id=1, source_target_pairs={{0,4},{2,6},{4,8},{6,10},{8,12},{10,14},{12,16},{14,18},{16,20},{1... | collective-permute-start | bytes 1179656 | tf_op jit(solution)/shard_map/ppermute | solution.py:18
  311.7 143.1 %collective-permute-start.5 = (bf16[384,512]{0,1:T(8,128)(2,1)}, bf16[384,512]{0,1:T(8,128)(2,1)}, u32[]{:S(2)}, u32[]{:S(2)}) collective-permute-start(bf16[384,512]{0,1:T(8,128)(2,1)} %bitcast.16), channel_id=1, source_target_pairs={{0,2},{2,4},{4,6},{6,8},{8,10},{10,12},{12,14},{14,16},{16,18},{18... | collective-permute-start | bytes 1179656 | tf_op jit(solution)/shard_map/ppermute | solution.py:18
  476.3 150.1 %all-gather.25.cloned.1.call-start = ((), (), s32[]{:S(2)}) async-start(), calls=%async_computation.7 | async-start | bytes 6193152 | tf_op jit(solution)/shard_map/all_gather | solution.py:85
  476.8 71.9 %copy-start.13 = (s32[2688]{0:T(1024)}, s32[2688]{0:T(1024)S(1)}, u32[]{:S(2)}) copy-start(s32[2688]{0:T(1024)S(1)} %add_select_fusion) | copy-start | bytes 32260
  570.3 182.2 %all-gather.21.cloned.1.call-start = ((), (), s32[]{:S(2)}) async-start(), calls=%async_computation.5 | async-start | bytes 2359296 | tf_op jit(solution)/shard_map/all_gather | solution.py:135
  639.3 25.4 %slice-start.3 = ((s8[5505024]{0:T(1024)(128)(4,1)}), s8[1310720]{0:T(1024)(128)(4,1)S(1)}, s32[]{:S(2)}) async-start(s8[5505024]{0:T(1024)(128)(4,1)} %bitcast.230), calls=%async_computation.11 | async-start | bytes 2621440
  649.2 15.6 %slice-start.4 = ((s8[5505024]{0:T(1024)(128)(4,1)}), s8[4194304]{0:T(1024)(128)(4,1)S(1)}, s32[]{:S(2)}) async-start(s8[5505024]{0:T(1024)(128)(4,1)} %bitcast.230), calls=%async_computation.12 | async-start | bytes 8388608
  656.9 37.3 %collective-permute-start.9 = (bf16[384,512]{0,1:T(8,128)(2,1)}, bf16[384,512]{0,1:T(8,128)(2,1)}, u32[]{:S(2)}, u32[]{:S(2)}) collective-permute-start(bf16[384,512]{0,1:T(8,128)(2,1)} %bitcast.51), channel_id=1, source_target_pairs={{0,6},{2,8},{4,10},{6,12},{8,14},{10,16},{12,18},{14,20},{16,22},{... | collective-permute-start | bytes 1179656 | tf_op jit(solution)/shard_map/ppermute | solution.py:18
  660.3 33.9 %collective-permute-start.10 = (bf16[384,512]{0,1:T(8,128)(2,1)}, bf16[384,512]{0,1:T(8,128)(2,1)}, u32[]{:S(2)}, u32[]{:S(2)}) collective-permute-start(bf16[384,512]{0,1:T(8,128)(2,1)} %bitcast.51), channel_id=1, source_target_pairs={{0,4},{2,6},{4,8},{6,10},{8,12},{10,14},{12,16},{14,18},{16,20},{1... | collective-permute-start | bytes 1179656 | tf_op jit(solution)/shard_map/ppermute | solution.py:18
  670.7 14.8 %collective-permute-start.6 = (bf16[384,512]{1,0:T(8,128)(2,1)}, bf16[384,512]{1,0:T(8,128)(2,1)S(1)}, u32[]{:S(2)}, u32[]{:S(2)}) collective-permute-start(bf16[384,512]{1,0:T(8,128)(2,1)} %fusion.46), channel_id=1, source_target_pairs={{0,6},{2,8},{4,10},{6,12},{8,14},{10,16},{12,18},{14,20},{16,22},{... | collective-permute-start | bytes 1179656 | tf_op jit(solution)/shard_map/ppermute | solution.py:18
  672.9 18.2 %collective-permute-start.7 = (bf16[384,512]{1,0:T(8,128)(2,1)}, bf16[384,512]{1,0:T(8,128)(2,1)}, u32[]{:S(2)}, u32[]{:S(2)}) collective-permute-start(bf16[384,512]{1,0:T(8,128)(2,1)} %fusion.46), channel_id=1, source_target_pairs={{0,4},{2,6},{4,8},{6,10},{8,12},{10,14},{12,16},{14,18},{16,20},{1... | collective-permute-start | bytes 1179656 | tf_op jit(solution)/shard_map/ppermute | solution.py:18
  677.0 14.0 %collective-permute-start.8 = (bf16[384,512]{1,0:T(8,128)(2,1)}, bf16[384,512]{1,0:T(8,128)(2,1)}, u32[]{:S(2)}, u32[]{:S(2)}) collective-permute-start(bf16[384,512]{1,0:T(8,128)(2,1)} %fusion.46), channel_id=1, source_target_pairs={{0,2},{2,4},{4,6},{6,8},{8,10},{10,12},{12,14},{14,16},{16,18},{18... | collective-permute-start | bytes 1179656 | tf_op jit(solution)/shard_map/ppermute | solution.py:18
  685.6 8.7 %collective-permute-start.11 = (bf16[384,512]{0,1:T(8,128)(2,1)}, bf16[384,512]{0,1:T(8,128)(2,1)}, u32[]{:S(2)}, u32[]{:S(2)}) collective-permute-start(bf16[384,512]{0,1:T(8,128)(2,1)} %bitcast.51), channel_id=1, source_target_pairs={{0,2},{2,4},{4,6},{6,8},{8,10},{10,12},{12,14},{14,16},{16,18},{18... | collective-permute-start | bytes 1179656 | tf_op jit(solution)/shard_map/ppermute | solution.py:18
  757.2 19.2 %copy-start = (bf16[384,2688]{1,0:T(8,128)(2,1)S(1)}, bf16[384,2688]{1,0:T(8,128)(2,1)}, u32[]{:S(2)}) copy-start(bf16[384,2688]{1,0:T(8,128)(2,1)} %add_convert_fusion.1) | copy-start | bytes 6193156
  (27 other events, 226.7 us)
Sparse Core Ops, SparseCore 0:
  8.9 58.6 all-gather.22
  69.9 90.7 all-gather.10
  163.0 106.7 all-gather.12
  271.2 124.8 all-gather.14
  397.5 121.8 all-gather.18
  520.8 27.1 all-gather.16
  570.4 55.9 all-gather.24
  715.5 36.9 all-gather.20
